TPU v7x, 32 devices: a whole 2x2x4 slice. The times are simulated.
32 devices in a mesh: rep: 4 (over z), col: 8 (over y, x, core).
Axes of the slice: x: 2, y: 2, z: 4, core: 2. Of those that a mesh axis runs over, the one named last changes fastest.
Arguments:
- acts: bfloat16 [8192, 4096], P('rep'), may hold values from -40 to 40
- cotangent: bfloat16 [8192, 8192], P('rep', 'col'), may hold values from -40 to 40
- weight: float32 [4096, 8192], P(('rep', 'col')), may hold values from -6 to 6
- moment: float32 [4096, 8192], P(('rep', 'col')), may hold values from -3 to 3
- second: float32 [4096, 8192], P(('rep', 'col')), may hold values from 0.25 to 4
Outputs:
- new_weight: float32 [4096, 8192], P(('rep', 'col'))
- new_moment: float32 [4096, 8192], P(('rep', 'col'))
- new_second: float32 [4096, 8192], P(('rep', 'col'))
- combined: float32 [4096, 8192], P(('rep', 'col'))
All inputs are finite; a program needn't handle non-finite values.
Results may differ from a plain program's by a relative error of at most 0.0003.
Values may be sent and summed in bfloat16 or wider, within the bound.
No kernel may reach another device: no remote copies, remote signals or barrier semaphores. Data moves between devices by JAX's collectives and lax.ppermute only.
A program may use at most 128 MiB of HBM per device.

v0:
```python
import jax
import jax.numpy as jnp
from jax import lax
from jax.sharding import PartitionSpec as P

bias_first = 0.9999734386011124
bias_second = 0.99407947077966


def swapped(block, axis, distance):
    count = lax.axis_size(axis)
    route = []
    for low in range(count):
        high = low | 1 << distance
        if high != low and high < count:
            route += [(low, high), (high, low)]
    return lax.ppermute(block, axis, route)


def split_half(segment, parity):
    folded = segment.reshape((segment.shape[0] // 2, 2) + segment.shape[1:])
    keeper = lax.dynamic_index_in_dim(folded, parity, 1, keepdims=False)
    giving = lax.dynamic_index_in_dim(folded, 1 - parity, 1, keepdims=False)
    return (keeper, giving)


def group_total(values, level):
    total = lax.psum(values, "col")
    for pairing in range(level + 1):
        total = total + swapped(total, "rep", pairing)
    return total


def halving_rows(acts, cotangent, replicas, levels, rep_rank):
    tokens_here, depth = acts.shape
    columns = cotangent.shape[1]
    block_rows = depth // replicas
    segment = None
    gradient = jnp.einsum("td,tc->dc", acts, cotangent, preferred_element_type=jnp.float32)
    segment = gradient.reshape(replicas, block_rows, columns)
    for level in range(levels):
        parity = rep_rank >> level & 1
        own_part, giving = split_half(segment, parity)
        peer_part = swapped(giving, "rep", level)
        own_sq = jnp.sum(own_part * own_part)
        peer_sq = jnp.sum(peer_part * peer_part)
        cross = jnp.sum(own_part * peer_part)
        lower_sq = jnp.where(parity == 0, own_sq, peer_sq)
        upper_sq = jnp.where(parity == 0, peer_sq, own_sq)
        totals = group_total(jnp.stack([lower_sq, upper_sq, cross]), level)
        own_total = jnp.where(parity == 0, totals[0], totals[1])
        peer_total = jnp.where(parity == 0, totals[1], totals[0])
        own_coef = 1.0 - totals[2] / (2.0 * (own_total + 1e-06))
        peer_coef = 1.0 - totals[2] / (2.0 * (peer_total + 1e-06))
        segment = own_coef * own_part + peer_coef * peer_part
    return segment.reshape(block_rows, columns)


def per_device(acts, cotangent, weight, moment, second):
    replicas = lax.axis_size("rep")
    levels = replicas.bit_length() - 1
    rep_rank = lax.axis_index("rep")
    reduced = halving_rows(acts, cotangent, replicas, levels, rep_rank)
    combined = lax.all_to_all(reduced, "col", split_axis=0, concat_axis=1, tiled=True)
    new_moment = 0.9 * moment + 0.1 * combined
    new_second = 0.95 * second + 0.05 * combined * combined
    update = new_moment / bias_first / (jnp.sqrt(new_second / bias_second) + 1e-08) + 0.1 * weight
    new_weight = weight - 0.0003 * update
    return (new_weight, new_moment, new_second, combined)


def solution(mesh):
    return jax.shard_map(
        per_device,
        mesh=mesh,
        in_specs=(
            P("rep", None),
            P("rep", "col"),
            P(("rep", "col"), None),
            P(("rep", "col"), None),
            P(("rep", "col"), None),
        ),
        out_specs=(
            P(("rep", "col"), None),
            P(("rep", "col"), None),
            P(("rep", "col"), None),
            P(("rep", "col"), None),
        ),
        check_vma=False,
    )
```

profile of v0, /device:TPU:0, one launch (start us, length us, event | category | flops | bytes accessed | tf_op | source)
XLA Modules:
  0.0 578.0 jit_solution(5947046217218718542)
XLA Ops:
  0.6 22.6 %fusion.7 = f32[4096,1024]{1,0:T(8,128)S(1)} fusion(bf16[2048,4096]{1,0:T(8,128)(2,1)} %param.5, bf16[2048,1024]{1,0:T(8,128)(2,1)} %param.6), kind=kOutput, calls=%fused_computation.21 | convolution fusion | flops 17179869184 | bytes 37748736 | tf_op jit(solution)/shard_map/td,tc->dc/dot_general | solution.py:39
  23.2 4.5 dynamic-slice_bitcast_fusion
  27.7 3.7 copy-done
  31.4 3.1 collective-permute-start
  34.5 180.8 %collective-permute-done = f32[2,1024,1024]{2,1,0:T(8,128)} collective-permute-done((f32[2,1024,1024]{2,1,0:T(8,128)}, f32[2,1024,1024]{2,1,0:T(8,128)}, u32[]{:S(2)}, u32[]{:S(2)}) %collective-permute-start) | collective-permute-done | bytes 8388640 | tf_op jit(solution)/shard_map/ppermute | solution.py:17
  215.2 7.5 %fusion = (f32[]{:T(128)}, f32[]{:T(128)}, f32[]{:T(128)}) fusion(f32[2,2,1024,1024]{3,2,1,0:T(8,128)} %bitcast.36, s32[]{:T(128)S(6)} %select_n.39, f32[2,1024,1024]{2,1,0:T(8,128)} %collective-permute-done), kind=kLoop, calls=%fused_computation.3 | loop fusion | flops 12582909 | bytes 16777232 | tf_op jit(solution)/shard_map/reduce_sum | solution.py:45
  225.4 0.7 pad_maximum_fusion
  226.1 13.0 %psum.14 = f32[3]{0:T(128)S(1)} all-reduce(f32[3]{0:T(128)S(1)} %pad_maximum_fusion), channel_id=1, replica_groups=mesh['rep'=4,'col'=8] {'col'}, use_global_device_ids=true, to_apply=%region_3.4 | all-reduce | flops 3 | bytes 24 | tf_op jit(solution)/shard_map/psum | solution.py:28
  239.1 1.6 collective-permute-start.1
  240.7 2.0 collective-permute-done.1
  247.2 12.1 %fusion.2 = f32[2,1024,1024]{2,1,0:T(8,128)} fusion(f32[2,1024,1024]{2,1,0:T(8,128)} %collective-permute-done, f32[2,2,1024,1024]{3,2,1,0:T(8,128)} %bitcast.37, s32[]{:T(128)S(6)} %select_n.39, f32[]{:T(128)S(6)} %sub.23, f32[]{:T(128)S(6)} %sub.22), kind=kLoop, calls=%fused_computation.5 | loop fusion | flops 6291456 | bytes 25165836 | tf_op jit(solution)/shard_map/add | solution.py:55
  259.2 4.8 constant_dynamic-slice_fusion
  264.0 2.6 collective-permute-start.2
  266.6 178.6 %collective-permute-done.2 = f32[1,1024,1024]{2,1,0:T(8,128)} collective-permute-done((f32[1,1024,1024]{2,1,0:T(8,128)}, f32[1,1024,1024]{2,1,0:T(8,128)}, u32[]{:S(2)}, u32[]{:S(2)}) %collective-permute-start.2) | collective-permute-done | bytes 4194336 | tf_op jit(solution)/shard_map/ppermute | solution.py:17
  445.2 5.2 multiply_reduce_fusion.3
  453.7 11.8 %psum.15 = f32[3]{0:T(128)S(1)} all-reduce(f32[3]{0:T(128)S(1)} %pad_maximum_fusion.1), channel_id=1, replica_groups=mesh['rep'=4,'col'=8] {'col'}, use_global_device_ids=true, to_apply=%region_7.8 | all-reduce | flops 3 | bytes 24 | tf_op jit(solution)/shard_map/psum | solution.py:28
  465.5 1.4 collective-permute-start.3
  466.9 2.2 collective-permute-done.3
  469.1 2.7 collective-permute-start.4
  471.8 1.8 collective-permute-done.4
  478.1 7.0 %multiply_add_fusion.1 = f32[1,1024,1024]{2,1,0:T(8,128)} fusion(f32[1,1024,1024]{2,1,0:T(8,128)} %collective-permute-done.2, f32[2,1024,1024]{2,1,0:T(8,128)} %fusion.2, s32[]{:T(128)S(6)} %select_n.45, f32[]{:T(128)S(6)} %sub.26, f32[]{:T(128)S(6)} %sub.25), kind=kLoop, calls=%fused_computation.12 | loop fusion | flops 3145728 | bytes 12582924 | tf_op jit(solution)/shard_map/add | solution.py:55
  485.0 4.7 all-to-all-start
  489.8 5.6 copy.11
  495.3 5.6 copy.13
  500.9 5.6 copy.9
  506.5 32.4 %all-to-all-done = f32[8,128,1024]{2,1,0:T(8,128)} async-done(((f32[8,128,1024]{2,1,0:T(8,128)}), f32[8,128,1024]{2,1,0:T(8,128)}, u32[]{:S(2)}, u32[]{:S(2)}) %all-to-all-start) | async-done | bytes 4194336 | tf_op jit(solution)/shard_map/all_to_all | solution.py:64
  538.9 5.3 copy.10
  544.2 11.4 %multiply_subtract_fusion = (f32[128,8192]{0,1:T(8,128)}, f32[128,8192]{0,1:T(8,128)}, f32[128,8192]{0,1:T(8,128)}) fusion(f32[128,8192]{0,1:T(8,128)} %copy.13, f32[128,8,1024]{0,2,1:T(8,128)} %copy.10, f32[128,8192]{0,1:T(8,128)} %copy.9, f32[128,8192]{0,1:T(8,128)} %copy.11), kind=kLoop, calls=%fused_computation.10 | loop fusion | flops 15728640 | bytes 29360128 | tf_op jit(solution)/shard_map/sub | solution.py:68
  555.6 5.6 copy.14
  561.2 5.6 copy.15
  566.8 5.6 copy.16
  572.4 5.6 copy.17
  (7 shorter events, 1.9 us)
Async XLA Ops:
  23.2 8.2 %copy-start = (f32[4096,1024]{1,0:T(8,128)}, f32[4096,1024]{1,0:T(8,128)S(1)}, u32[]{:S(2)}) copy-start(f32[4096,1024]{1,0:T(8,128)S(1)} %fusion.7) | copy-start | bytes 50331652
  31.4 183.8 %collective-permute-start = (f32[2,1024,1024]{2,1,0:T(8,128)}, f32[2,1024,1024]{2,1,0:T(8,128)}, u32[]{:S(2)}, u32[]{:S(2)}) collective-permute-start(f32[2,1024,1024]{2,1,0:T(8,128)} %dynamic-slice_bitcast_fusion), channel_id=1, source_target_pairs={{0,8},{8,0},{16,24},{24,16},{1,9},{9,1},{17,25},{25,17},{2,10},{10... | collective-permute-start | bytes 25165832 | tf_op jit(solution)/shard_map/ppermute | solution.py:17
  239.1 3.6 collective-permute-start.1
  264.0 181.2 %collective-permute-start.2 = (f32[1,1024,1024]{2,1,0:T(8,128)}, f32[1,1024,1024]{2,1,0:T(8,128)}, u32[]{:S(2)}, u32[]{:S(2)}) collective-permute-start(f32[1,1024,1024]{2,1,0:T(8,128)} %constant_dynamic-slice_fusion), channel_id=1, source_target_pairs={{0,16},{16,0},{8,24},{24,8},{1,17},{17,1},{9,25},{25,9},{2,18},{18... | collective-permute-start | bytes 12582920 | tf_op jit(solution)/shard_map/ppermute | solution.py:17
  465.5 3.6 collective-permute-start.3
  469.1 4.5 collective-permute-start.4
  485.0 53.8 %all-to-all-start = ((f32[8,128,1024]{2,1,0:T(8,128)}), f32[8,128,1024]{2,1,0:T(8,128)}, u32[]{:S(2)}, u32[]{:S(2)}) async-start(f32[8,128,1024]{2,1,0:T(8,128)} %bitcast.38), calls=%async_computation | async-start | bytes 8388608 | tf_op jit(solution)/shard_map/all_to_all | solution.py:64
where the time goes:
time: 579 us; the launch traced here: 578 us
  waiting for transfers between devices  398 us (69%)
  local copies, waits for them, and re-layouts  58.6 us (10%)
  other arithmetic  44.6 us (8%)
  blocking collectives  24.7 us (4%)
  matrix products  22.6 us (4%)
  starting transfers between devices  16.1 us (3%)
  between operations  13.7 us (2%)
    ppermute x5, waiting for transfers between devices, swapped(): return lax.ppermute(block, axis, route)  365 us
    unnamed x9, local copies, waits for them, and re-layouts  42.8 us
    all_to_all x1, waiting for transfers between devices, per_device(): lax.all_to_all(reduced, 'col', split_axis=0, concat_axis=1, tiled=True)  32.4 us
    psum x2, blocking collectives, group_total(): total = lax.psum(values, 'col')  24.7 us
    dot_general x1, matrix products, halving_rows(): jnp.einsum('td,tc->dc', acts, cotangent, preferred_element_type=jnp.float32)  22.6 us
    add x2, other arithmetic, halving_rows(): segment = own_coef * own_part + peer_coef * peer_part  19 us
    reduce_sum x2, other arithmetic, halving_rows(): own_sq = jnp.sum(own_part * own_part)  12.7 us
  transfers between devices with their start and end apart: 6, of which 6 were waited for; matrix products, arithmetic and copies ran while one was open for 3% of the time, Pallas kernels for 0%

commit v1 on v0

--- a/solution.py
+++ b/solution.py
@@ -5,6 +5,22 @@
 
 bias_first = 0.9999734386011124
 bias_second = 0.99407947077966
+
+
+def pairwise_exchange(x, axis, split, join):
+    ways, here = (lax.axis_size(axis), lax.axis_index(axis))
+    width = x.shape[split] // ways
+    dims = list(x.shape)
+    dims[split] = width
+    height = dims[join]
+    dims[join] = height * ways
+    full = jnp.zeros(dims, x.dtype)
+    for mask in range(ways):
+        part = lax.dynamic_slice_in_dim(x, (here ^ mask) * width, width, axis=split)
+        if mask:
+            part = lax.ppermute(part, axis, [(d, d ^ mask) for d in range(ways)])
+        full = lax.dynamic_update_slice_in_dim(full, part, (here ^ mask) * height, axis=join)
+    return full
 
 
 def swapped(block, axis, distance):
@@ -61,7 +77,7 @@
     levels = replicas.bit_length() - 1
     rep_rank = lax.axis_index("rep")
     reduced = halving_rows(acts, cotangent, replicas, levels, rep_rank)
-    combined = lax.all_to_all(reduced, "col", split_axis=0, concat_axis=1, tiled=True)
+    combined = pairwise_exchange(reduced, "col", 0, 1)
     new_moment = 0.9 * moment + 0.1 * combined
     new_second = 0.95 * second + 0.05 * combined * combined
     update = new_moment / bias_first / (jnp.sqrt(new_second / bias_second) + 1e-08) + 0.1 * weight

time: 579 us -> 542 us (0.936)
  local copies, waits for them, and re-layouts: 58.6 us -> 24.2 us
  other arithmetic: 44.6 us -> 36.6 us
    unnamed x9 -> x12, local copies, waits for them, and re-layouts: 42.8 us -> 5.75 us
    ppermute x0 -> x7, waiting for transfers between devices: none -> 36.8 us  [pairwise_exchange(): part = lax.ppermute(part, axis, [(d, d ^ mask) for d in range(ways)])]
    all_to_all x1 -> x0, waiting for transfers between devices: 32.4 us -> none  [per_device(): lax.all_to_all(reduced, 'col', split_axis=0, concat_axis=1, tiled=True)]
    dynamic_update_slice x0 -> x8, local copies, waits for them, and re-layouts: none -> 6.53 us  [pairwise_exchange(): lax.dynamic_update_slice_in_dim(full, part, (here ^ mask) * height, axis=...]
  transfers between devices with their start and end apart: 6 -> 12, of which waited for: 6 -> 8; matrix products, arithmetic and copies ran while one was open for 3% -> 1% of each run, Pallas kernels for 0% -> 0%
where the time goes in v1:
time: 542 us; the launch traced here: 541 us
  waiting for transfers between devices  402 us (74%)
  other arithmetic  36.6 us (7%)
  blocking collectives  24.9 us (5%)
  local copies, waits for them, and re-layouts  24.2 us (4%)
  matrix products  22.6 us (4%)
  starting transfers between devices  16.4 us (3%)
  between operations  13.8 us (3%)
    ppermute x5, waiting for transfers between devices, swapped(): return lax.ppermute(block, axis, route)  365 us
    ppermute x7, waiting for transfers between devices, pairwise_exchange(): part = lax.ppermute(part, axis, [(d, d ^ mask) for d in range(ways)])  36.8 us
    psum x2, blocking collectives, group_total(): total = lax.psum(values, 'col')  24.9 us
    dot_general x1, matrix products, halving_rows(): jnp.einsum('td,tc->dc', acts, cotangent, preferred_element_type=jnp.float32)  22.6 us
    add x2, other arithmetic, halving_rows(): segment = own_coef * own_part + peer_coef * peer_part  16.5 us
    reduce_sum x2, other arithmetic, halving_rows(): own_sq = jnp.sum(own_part * own_part)  12.7 us
    ppermute x5, starting transfers between devices, swapped(): return lax.ppermute(block, axis, route)  11.4 us
  transfers between devices with their start and end apart: 12, of which 8 were waited for; matrix products, arithmetic and copies ran while one was open for 1% of the time, Pallas kernels for 0%

profile of v1, /device:TPU:0, one launch (start us, length us, event | category | flops | bytes accessed | tf_op | source)
XLA Modules:
  0.0 540.8 jit_solution(6521635939980908042)
XLA Ops:
  0.6 22.6 %fusion.7 = f32[4096,1024]{1,0:T(8,128)S(1)} fusion(bf16[2048,4096]{1,0:T(8,128)(2,1)} %param.5, bf16[2048,1024]{1,0:T(8,128)(2,1)} %param.6), kind=kOutput, calls=%fused_computation.36 | convolution fusion | flops 17179869184 | bytes 37748736 | tf_op jit(solution)/shard_map/td,tc->dc/dot_general | solution.py:55
  23.2 4.5 dynamic-slice_bitcast_fusion
  27.7 3.7 copy-done
  31.4 3.1 collective-permute-start
  34.5 180.8 %collective-permute-done = f32[2,1024,1024]{2,1,0:T(8,128)} collective-permute-done((f32[2,1024,1024]{2,1,0:T(8,128)}, f32[2,1024,1024]{2,1,0:T(8,128)}, u32[]{:S(2)}, u32[]{:S(2)}) %collective-permute-start) | collective-permute-done | bytes 8388640 | tf_op jit(solution)/shard_map/ppermute | solution.py:33
  215.2 7.5 %fusion = (f32[]{:T(128)}, f32[]{:T(128)}, f32[]{:T(128)}) fusion(f32[2,2,1024,1024]{3,2,1,0:T(8,128)} %bitcast.44, s32[]{:T(128)S(6)} %select_n.87, f32[2,1024,1024]{2,1,0:T(8,128)} %collective-permute-done), kind=kLoop, calls=%fused_computation.3 | loop fusion | flops 12582909 | bytes 16777232 | tf_op jit(solution)/shard_map/reduce_sum | solution.py:61
  226.1 13.0 %psum.14 = f32[3]{0:T(128)S(1)} all-reduce(f32[3]{0:T(128)S(1)} %pad_maximum_fusion), channel_id=1, replica_groups=mesh['rep'=4,'col'=8] {'col'}, use_global_device_ids=true, to_apply=%region_3.4 | all-reduce | flops 3 | bytes 24 | tf_op jit(solution)/shard_map/psum | solution.py:44
  239.1 1.6 collective-permute-start.1
  240.7 2.0 collective-permute-done.1
  247.2 12.1 %fusion.2 = f32[2,1024,1024]{2,1,0:T(8,128)} fusion(f32[2,1024,1024]{2,1,0:T(8,128)} %collective-permute-done, f32[2,2,1024,1024]{3,2,1,0:T(8,128)} %bitcast.45, s32[]{:T(128)S(6)} %select_n.87, f32[]{:T(128)S(6)} %sub.23, f32[]{:T(128)S(6)} %sub.22), kind=kLoop, calls=%fused_computation.5 | loop fusion | flops 6291456 | bytes 25165836 | tf_op jit(solution)/shard_map/add | solution.py:71
  259.2 4.8 constant_dynamic-slice_fusion
  264.0 2.6 collective-permute-start.2
  266.6 178.6 %collective-permute-done.2 = f32[1,1024,1024]{2,1,0:T(8,128)} collective-permute-done((f32[1,1024,1024]{2,1,0:T(8,128)}, f32[1,1024,1024]{2,1,0:T(8,128)}, u32[]{:S(2)}, u32[]{:S(2)}) %collective-permute-start.2) | collective-permute-done | bytes 4194336 | tf_op jit(solution)/shard_map/ppermute | solution.py:33
  445.2 5.2 multiply_reduce_fusion.3
  453.7 12.0 %psum.15 = f32[3]{0:T(128)S(1)} all-reduce(f32[3]{0:T(128)S(1)} %pad_maximum_fusion.1), channel_id=1, replica_groups=mesh['rep'=4,'col'=8] {'col'}, use_global_device_ids=true, to_apply=%region_7.8 | all-reduce | flops 3 | bytes 24 | tf_op jit(solution)/shard_map/psum | solution.py:44
  465.7 1.4 collective-permute-start.3
  467.1 2.2 collective-permute-done.3
  469.3 2.7 collective-permute-start.4
  472.0 1.8 collective-permute-done.4
  478.3 4.5 multiply_add_fusion.1
  482.7 2.0 copy-done.2
  485.8 1.9 collective-permute-start.7
  487.7 1.6 collective-permute-start.8
  489.7 1.3 bitcast_dynamic-update-slice_fusion
  491.0 1.2 collective-permute-start.10
  492.3 1.8 constant_dynamic-update-slice_fusion.6
  494.1 6.6 %collective-permute-done.6 = f32[128,1024]{1,0:T(8,128)} collective-permute-done((f32[128,1024]{1,0:T(8,128)S(1)}, f32[128,1024]{1,0:T(8,128)}, u32[]{:S(2)}, u32[]{:S(2)}) %collective-permute-start.6) | collective-permute-done | bytes 524320 | tf_op jit(solution)/shard_map/ppermute | solution.py:21
  502.2 8.8 %collective-permute-done.7 = f32[128,1024]{1,0:T(8,128)} collective-permute-done((f32[128,1024]{1,0:T(8,128)S(1)}, f32[128,1024]{1,0:T(8,128)}, u32[]{:S(2)}, u32[]{:S(2)}) %collective-permute-start.7) | collective-permute-done | bytes 524320 | tf_op jit(solution)/shard_map/ppermute | solution.py:21
  511.0 1.1 constant_dynamic-update-slice_fusion.4
  512.1 1.1 constant_dynamic-update-slice_fusion.3
  513.2 21.4 %collective-permute-done.9 = f32[128,1024]{1,0:T(8,128)S(1)} collective-permute-done((f32[128,1024]{1,0:T(8,128)S(1)}, f32[128,1024]{1,0:T(8,128)S(1)}, u32[]{:S(2)}, u32[]{:S(2)}) %collective-permute-start.9) | collective-permute-done | bytes 524320 | tf_op jit(solution)/shard_map/ppermute | solution.py:21
  534.8 6.0 %multiply_subtract_fusion = (f32[128,8192]{1,0:T(8,128)}, f32[128,8192]{1,0:T(8,128)}, f32[128,8192]{1,0:T(8,128)}) fusion(f32[128,8192]{1,0:T(8,128)S(1)} %copy-done.3, f32[128,8192]{1,0:T(8,128)S(1)} %constant_dynamic-update-slice_fusion, f32[128,8192]{1,0:T(8,128)S(1)} %copy-done.4, f32[128,8192]{1,0:T(8,128)S(1)} %copy-done.5), kind=kLoop, calls=%fused_computation.10 | loop fusion | flops 15728640 | bytes 29360128 | tf_op jit(solution)/shard_map/sub | solution.py:84
  (31 shorter events, 5.8 us)
Async XLA Ops:
  23.2 8.2 %copy-start = (f32[4096,1024]{1,0:T(8,128)}, f32[4096,1024]{1,0:T(8,128)S(1)}, u32[]{:S(2)}) copy-start(f32[4096,1024]{1,0:T(8,128)S(1)} %fusion.7) | copy-start | bytes 50331652
  31.4 183.8 %collective-permute-start = (f32[2,1024,1024]{2,1,0:T(8,128)}, f32[2,1024,1024]{2,1,0:T(8,128)}, u32[]{:S(2)}, u32[]{:S(2)}) collective-permute-start(f32[2,1024,1024]{2,1,0:T(8,128)} %dynamic-slice_bitcast_fusion), channel_id=1, source_target_pairs={{0,8},{8,0},{16,24},{24,16},{1,9},{9,1},{17,25},{25,17},{2,10},{10... | collective-permute-start | bytes 25165832 | tf_op jit(solution)/shard_map/ppermute | solution.py:33
  239.1 3.6 collective-permute-start.1
  264.0 181.2 %collective-permute-start.2 = (f32[1,1024,1024]{2,1,0:T(8,128)}, f32[1,1024,1024]{2,1,0:T(8,128)}, u32[]{:S(2)}, u32[]{:S(2)}) collective-permute-start(f32[1,1024,1024]{2,1,0:T(8,128)} %constant_dynamic-slice_fusion), channel_id=1, source_target_pairs={{0,16},{16,0},{8,24},{24,8},{1,17},{17,1},{9,25},{25,9},{2,18},{18... | collective-permute-start | bytes 12582920 | tf_op jit(solution)/shard_map/ppermute | solution.py:33
  465.7 3.6 collective-permute-start.3
  469.3 4.5 collective-permute-start.4
  482.7 2.0 copy-start.2
  485.8 5.2 collective-permute-start.5
  485.8 14.9 %collective-permute-start.6 = (f32[128,1024]{1,0:T(8,128)S(1)}, f32[128,1024]{1,0:T(8,128)}, u32[]{:S(2)}, u32[]{:S(2)}) collective-permute-start(f32[128,1024]{1,0:T(8,128)S(1)} %get-tuple-element.18), channel_id=1, source_target_pairs={{0,2},{1,3},{2,0},{3,1},{4,6},{5,7},{6,4},{7,5},{8,10},{9,11},{10,... | collective-permute-start | bytes 1572872 | tf_op jit(solution)/shard_map/ppermute | solution.py:21
  485.8 25.2 %collective-permute-start.7 = (f32[128,1024]{1,0:T(8,128)S(1)}, f32[128,1024]{1,0:T(8,128)}, u32[]{:S(2)}, u32[]{:S(2)}) collective-permute-start(f32[128,1024]{1,0:T(8,128)S(1)} %get-tuple-element.17), channel_id=1, source_target_pairs={{0,3},{1,2},{2,1},{3,0},{4,7},{5,6},{6,5},{7,4},{8,11},{9,10},{10,... | collective-permute-start | bytes 1572872 | tf_op jit(solution)/shard_map/ppermute | solution.py:21
  487.7 24.4 %collective-permute-start.8 = (f32[128,1024]{1,0:T(8,128)S(1)}, f32[128,1024]{1,0:T(8,128)}, u32[]{:S(2)}, u32[]{:S(2)}) collective-permute-start(f32[128,1024]{1,0:T(8,128)S(1)} %get-tuple-element.16), channel_id=1, source_target_pairs={{0,4},{1,5},{2,6},{3,7},{4,0},{5,1},{6,2},{7,3},{8,12},{9,13},{10,... | collective-permute-start | bytes 1572872 | tf_op jit(solution)/shard_map/ppermute | solution.py:21
  489.2 45.3 %collective-permute-start.9 = (f32[128,1024]{1,0:T(8,128)S(1)}, f32[128,1024]{1,0:T(8,128)S(1)}, u32[]{:S(2)}, u32[]{:S(2)}) collective-permute-start(f32[128,1024]{1,0:T(8,128)S(1)} %get-tuple-element.15), channel_id=1, source_target_pairs={{0,5},{1,4},{2,7},{3,6},{4,1},{5,0},{6,3},{7,2},{8,13},{9,12},{10,... | collective-permute-start | bytes 1572872 | tf_op jit(solution)/shard_map/ppermute | solution.py:21
  489.3 45.5 %copy-start.5 = (f32[128,8192]{1,0:T(8,128)S(1)}, f32[128,8192]{1,0:T(8,128)}, u32[]{:S(2)}) copy-start(f32[128,8192]{1,0:T(8,128)} %param.9) | copy-start | bytes 12582916
  489.7 45.1 %copy-start.3 = (f32[128,8192]{1,0:T(8,128)S(1)}, f32[128,8192]{1,0:T(8,128)}, u32[]{:S(2)}) copy-start(f32[128,8192]{1,0:T(8,128)} %param.7) | copy-start | bytes 12582916
  489.7 45.1 %copy-start.4 = (f32[128,8192]{1,0:T(8,128)S(1)}, f32[128,8192]{1,0:T(8,128)}, u32[]{:S(2)}) copy-start(f32[128,8192]{1,0:T(8,128)} %param.8) | copy-start | bytes 12582916
  491.0 43.6 %collective-permute-start.10 = (f32[128,1024]{1,0:T(8,128)S(1)}, f32[128,1024]{1,0:T(8,128)S(1)}, u32[]{:S(2)}, u32[]{:S(2)}) collective-permute-start(f32[128,1024]{1,0:T(8,128)S(1)} %get-tuple-element.14), channel_id=1, source_target_pairs={{0,6},{1,7},{2,4},{3,5},{4,2},{5,3},{6,0},{7,1},{8,14},{9,15},{10,... | collective-permute-start | bytes 1572872 | tf_op jit(solution)/shard_map/ppermute | solution.py:21
  500.7 34.0 %collective-permute-start.11 = (f32[128,1024]{1,0:T(8,128)S(1)}, f32[128,1024]{1,0:T(8,128)S(1)}, u32[]{:S(2)}, u32[]{:S(2)}) collective-permute-start(f32[128,1024]{1,0:T(8,128)S(1)} %get-tuple-element.13), channel_id=1, source_target_pairs={{0,7},{1,6},{2,5},{3,4},{4,3},{5,2},{6,1},{7,0},{8,15},{9,14},{10,... | collective-permute-start | bytes 1572872 | tf_op jit(solution)/shard_map/ppermute | solution.py:21
  534.8 6.0 %copy-start.1 = (f32[128,8192]{1,0:T(8,128)}, f32[128,8192]{1,0:T(8,128)S(1)}, u32[]{:S(2)}) copy-start(f32[128,8192]{1,0:T(8,128)S(1)} %constant_dynamic-update-slice_fusion) | copy-start | bytes 12582916
